TPU v7x, 512 devices: a whole 4x4x16 slice. The times are simulated.
512 devices in a mesh: section: 8 (over z_lo), dp: 64 (over z_hi, x, y, core).
Axes of the slice: x: 4, y: 4, z: 16 (z_hi: 2, z_lo: 8; z = z_hi * 8 + z_lo), core: 2. Of those that a mesh axis runs over, the one named last changes fastest.
Arguments:
- patches: bfloat16 [8, 8192, 2048], P('section', 'dp'), may hold values from -6 to 6
- pack_dest: int32 [8, 8192], P('section', 'dp'), may hold values from 0 to 8191, as said below
- seg_ids: int32 [8, 8192], P('section', 'dp'), may hold values from 0 to 191, as said below
- w_patch_in: bfloat16 [8, 2048, 256], P('section', 'dp'), may hold values from -0.125 to 0.125
- w_patch_out: bfloat16 [8, 256, 2048], P('section', 'dp'), may hold values from -0.375 to 0.375
- w_query: bfloat16 [8, 2048, 1024], P('section', 'dp')
- w_keyval: bfloat16 [8, 2048, 512], P('section', 'dp')
- w_attn_out: bfloat16 [8, 1024, 2048], P('section', 'dp'), may hold values from -0.75 to 0.75
Outputs:
- handed: bfloat16 [8, 8192, 2048], P('section', 'dp')
Inputs may be any that keep to these rules, and one draw needn't show every extreme that they name: For each micro-batch a permutation of the 8192 rows; the rows i of one aligned block of 128 rows send at most 4 rows into any one aligned block of pack_dest values, and some pair of blocks reaches 4. `seg_ids`: never falling along a micro-batch's rows, starting at 0 and rising by one where a document starts; a document starts at row 0, at every row r with r % 64 == 32, and in exactly 63 of the spans between two such rows at one other row, never at a multiple of 64; each document has 1 to 64 rows and one has exactly 64.
All inputs are finite; a program needn't handle non-finite values.
Results may differ from a plain program's by a relative error of at most 0.015.
The roundings to bfloat16 on the way count: a program that leaves them out, or rounds other values in their place, can miss the bound.
Values may be sent and summed in bfloat16 or wider, within the bound.
A program may use at most 64 MiB of HBM per device.

v0:
```python
import math

import jax
import jax.numpy as jnp
from jax import lax
from jax.sharding import PartitionSpec as P

HEADS = 16
KV_HEADS = 4
HEAD_WIDTH = 64


def shifted(block, axis, distance):
    devices = range(lax.axis_size(axis))
    route = [(i - distance, i) for i in devices if i - distance in devices]
    return lax.ppermute(block, axis, route)


def from_behind(x, axis, by):
    devices = lax.axis_size(axis)
    return lax.ppermute(x, axis, [(i, (i + by) % devices) for i in range(devices)])


def fold_columns(left, shard_piece):
    return jnp.dot(left, shard_piece, preferred_element_type=jnp.float32)


def embed_rows(hidden, w_out):
    summed = fold_columns(hidden, lax.all_gather(w_out, "dp", axis=0, tiled=True))
    return summed.astype(jnp.bfloat16)


def send_buffers(values, dest_rows, devices):
    row_count = values.shape[0]
    capacity = 2 * row_count // devices
    dest_device = dest_rows // row_count
    dest_slot = dest_rows % row_count
    one_hot = (dest_device[:, None] == jnp.arange(devices, dtype=jnp.int32)[None, :]).astype(
        jnp.int32
    )
    earlier = jnp.cumsum(one_hot, axis=0) - one_hot
    rank_in = jnp.sum(earlier * one_hot, axis=1)
    flat_slot = dest_device * capacity + rank_in
    buffer = (
        jnp.zeros((devices * capacity, values.shape[1]), values.dtype).at[flat_slot].set(values)
    )
    places = jnp.full((devices * capacity,), row_count, jnp.int32).at[flat_slot].set(dest_slot)
    return (buffer.reshape(devices, capacity, values.shape[1]), places.reshape(devices, capacity))


def place_rows(received, places, row_count):
    width = received.shape[-1]
    target = jnp.zeros((row_count, width), received.dtype)
    return target.at[places.reshape(-1)].set(received.reshape(-1, width), mode="drop")


def attend_rows(queries, keyval, query_seg, key_seg, query_pos, key_pos):
    row_count = queries.shape[0]
    key_count = keyval.shape[0]
    repeat = HEADS // KV_HEADS
    kv_width = KV_HEADS * HEAD_WIDTH
    per_head_queries = queries.reshape(row_count, KV_HEADS, repeat, HEAD_WIDTH)
    per_head_keys = keyval[:, :kv_width].reshape(key_count, KV_HEADS, HEAD_WIDTH)
    per_head_values = keyval[:, kv_width:].reshape(key_count, KV_HEADS, HEAD_WIDTH)
    attention_logits = jnp.einsum(
        "jiyp,aip->iyja", per_head_queries, per_head_keys, preferred_element_type=jnp.float32
    ) / math.sqrt(HEAD_WIDTH)
    allowed = (
        (query_seg[:, None] == key_seg[None, :])
        & (key_pos[None, :] >= 0)
        & (key_pos[None, :] <= query_pos[:, None])
    )
    attention_logits = jnp.where(allowed[None, None], attention_logits, -jnp.inf)
    row_max = jnp.max(attention_logits, axis=-1, keepdims=True)
    expon = jnp.exp(attention_logits - row_max)
    attention_probabilities = (expon / jnp.sum(expon, axis=-1, keepdims=True)).astype(jnp.bfloat16)
    attended_values = jnp.einsum(
        "iolf,fia->lioa",
        attention_probabilities,
        per_head_values,
        preferred_element_type=jnp.float32,
    )
    return attended_values.astype(jnp.bfloat16).reshape(row_count, HEADS * HEAD_WIDTH)


def on_device(patches, pack_dest, seg_ids, w_patch_in, w_patch_out, w_query, w_keyval, w_attn_out):
    devices = lax.axis_size("dp")
    raw_rows = patches[0]
    row_count = raw_rows.shape[0]
    first_layer = fold_columns(raw_rows, lax.all_gather(w_patch_in[0], "dp", axis=0, tiled=True))
    hidden = jax.nn.gelu(first_layer).astype(jnp.bfloat16)
    outgoing, places = send_buffers(embed_rows(hidden, w_patch_out[0]), pack_dest[0], devices)
    received, got_places = (
        lax.all_to_all(outgoing, "dp", split_axis=0, concat_axis=0, tiled=True),
        lax.all_to_all(places, "dp", split_axis=0, concat_axis=0, tiled=True),
    )
    packed = place_rows(received, got_places, row_count)
    residual = packed.astype(jnp.float32)
    normed = (
        residual * lax.rsqrt(jnp.mean(residual * residual, axis=-1, keepdims=True) + 1e-05)
    ).astype(jnp.bfloat16)
    queries = fold_columns(normed, lax.all_gather(w_query[0], "dp", axis=0, tiled=True)).astype(
        jnp.bfloat16
    )
    keyval = fold_columns(normed, lax.all_gather(w_keyval[0], "dp", axis=0, tiled=True)).astype(
        jnp.bfloat16
    )
    segment = seg_ids[0]
    own_pos = lax.axis_index("dp") * row_count + jnp.arange(row_count, dtype=jnp.int32)
    prev_kv, prev_seg = shifted((keyval, segment), "dp", 1)
    prev_pos = own_pos - row_count
    attended_values = attend_rows(
        queries,
        jnp.concatenate([prev_kv, keyval], axis=0),
        segment,
        jnp.concatenate([prev_seg, segment], axis=0),
        own_pos,
        jnp.concatenate([prev_pos, own_pos], axis=0),
    )
    projected = fold_columns(
        attended_values, lax.all_gather(w_attn_out[0], "dp", axis=0, tiled=True)
    )
    layer_out = (projected + residual).astype(jnp.bfloat16)
    handed = from_behind(layer_out, "section", 1)
    return handed[None]


def solution(mesh):
    in_specs = (
        P("section", "dp", None),
        P("section", "dp"),
        P("section", "dp"),
        P("section", "dp", None),
        P("section", "dp", None),
        P("section", "dp", None),
        P("section", "dp", None),
        P("section", "dp", None),
    )
    out_specs = P("section", "dp", None)
    return jax.shard_map(
        on_device, mesh=mesh, in_specs=in_specs, out_specs=out_specs, check_vma=False
    )
```

profile of v0, /device:TPU:1, one launch (start us, length us, event | category | flops | bytes accessed | tf_op | source)
XLA Modules:
  0.0 641.6 jit_solution(8412972978179343891)
XLA Ops:
  6.5 0.0 copy-start
  6.5 0.0 all-gather.13.cloned.1.call-start
  6.5 1.4 copy.24
  7.9 0.0 all-gather.13.cloned.1.call-update
  8.0 0.0 all-gather.11.cloned.1.call-start
  8.0 0.7 all-gather.11.cloned.1.call-update
  8.7 0.0 all-gather.15.cloned.1.call-start
  8.8 0.7 all-gather.15.cloned.1.call-update
  9.5 0.0 all-gather.17.cloned.1.call-start
  9.5 0.5 all-gather.17.cloned.1.call-update
  10.0 0.0 all-gather.19.cloned.1.call-start
  10.1 0.5 all-gather.19.cloned.1.call-update
  10.6 0.7 and_select_fusion
  11.3 0.1 fusion.63
  11.4 0.2 reduce_window_sum.11
  11.5 0.2 select_reduce_fusion
  11.7 0.7 fusion.64
  12.4 1.0 scatter_custom_fusion
  13.4 0.7 all_to_all.9
  14.1 22.2 %all-to-all-start = ((s32[64,1,4]{2,1,0:T(1,128)}), s32[64,1,4]{2,1,0:T(1,128)S(1)}, u32[]{:S(2)}, u32[]{:S(2)}) async-start(s32[64,1,4]{2,1,0:T(1,128)} %bitcast.4), calls=%async_computation | async-start | bytes 65536 | tf_op jit(solution)/shard_map/all_to_all | solution.py:95
  36.4 94.1 %all-gather.13.cloned.1.call-done = bf16[1,256,2048]{2,0,1:T(2,128)(2,1)} async-done(((bf16[1,4,2048]{2,0,1:T(2,128)(2,1)}), bf16[1,256,2048]{2,0,1:T(2,128)(2,1)}) %all-gather.13.cloned.1.call-update) | async-done | bytes 1048592 | tf_op jit(solution)/shard_map/all_gather | solution.py:29
  130.5 97.0 %all-gather.11.cloned.1.call-done = bf16[1,2048,256]{2,1,0:T(8,128)(2,1)} async-done(((bf16[1,32,256]{2,1,0:T(8,128)(2,1)}), bf16[1,2048,256]{2,1,0:T(8,128)(2,1)}) %all-gather.11.cloned.1.call-update) | async-done | bytes 1048592 | tf_op jit(solution)/shard_map/all_gather | solution.py:90
  227.5 0.0 copy-done
  227.5 3.0 convolution_convert_fusion
  230.4 1.7 scatter_custom_fusion.1
  232.2 0.0 copy-start.1
  232.2 1.2 reshape.254
  233.4 0.0 all-to-all-done
  233.4 5.0 all-to-all-start.1
  238.5 0.0 copy-done.1
  238.5 3.5 collective-permute-start.1
  242.1 0.6 collective-permute-done.1
  242.7 0.5 broadcast.234
  243.2 0.7 reduce.3
  244.0 0.1 reshape.253
  244.1 29.6 %all-to-all-done.1 = bf16[64,4,2048]{2,1,0:T(4,128)(2,1)S(1)} async-done(((bf16[64,4,2048]{2,1,0:T(4,128)(2,1)}), bf16[64,4,2048]{2,1,0:T(4,128)(2,1)S(1)}, u32[]{:S(2)}, u32[]{:S(2)}) %all-to-all-start.1) | async-done | bytes 1048608 | tf_op jit(solution)/shard_map/all_to_all | solution.py:94
  273.6 0.3 reshape.280
  273.9 2.2 scatter_custom_fusion.2
  276.1 0.2 fusion.20
  276.3 80.0 %all-gather.15.cloned.1.call-done = bf16[1,2048,512]{2,1,0:T(8,128)(2,1)} async-done(((bf16[1,32,512]{2,1,0:T(8,128)(2,1)}), bf16[1,2048,512]{2,1,0:T(8,128)(2,1)}) %all-gather.15.cloned.1.call-update) | async-done | bytes 2097168 | tf_op jit(solution)/shard_map/all_gather | solution.py:105
  356.3 2.1 fusion.17
  358.4 2.0 collective-permute-start
  360.4 0.2 compare_and_fusion
  360.6 1.7 collective-permute-done
  362.3 0.1 copy.26
  362.4 0.1 copy.25
  362.5 120.1 %all-gather.17.cloned.1.call-done = bf16[1,2048,1024]{2,1,0:T(8,128)(2,1)} async-done(((bf16[1,32,1024]{2,1,0:T(8,128)(2,1)}), bf16[1,2048,1024]{2,1,0:T(8,128)(2,1)}) %all-gather.17.cloned.1.call-update) | async-done | bytes 4194320 | tf_op jit(solution)/shard_map/all_gather | solution.py:102
  482.7 2.9 fusion.14
  485.6 0.2 copy.27
  485.8 0.8 fusion.77
  486.6 1.1 convolution_convert_fusion.1
  487.7 121.9 %all-gather.19.cloned.1.call-done = bf16[1,1024,2048]{2,1,0:T(8,128)(2,1)} async-done(((bf16[1,16,2048]{2,1,0:T(8,128)(2,1)}), bf16[1,1024,2048]{2,1,0:T(8,128)(2,1)}) %all-gather.19.cloned.1.call-update) | async-done | bytes 4194320 | tf_op jit(solution)/shard_map/all_gather | solution.py:121
  609.6 2.9 fusion.8
  612.5 1.9 collective-permute-start.2
  614.5 19.8 %collective-permute-done.2 = bf16[128,2048]{1,0:T(8,128)(2,1)S(1)} collective-permute-done((bf16[128,2048]{1,0:T(8,128)(2,1)S(1)}, bf16[128,2048]{1,0:T(8,128)(2,1)S(1)}, u32[]{:S(2)}, u32[]{:S(2)}) %collective-permute-start.2) | collective-permute-done | bytes 524320 | tf_op jit(solution)/shard_map/ppermute | solution.py:21
  634.3 0.8 copy.38
  (8 shorter events, 0.1 us)
Async XLA Ops:
  6.5 220.9 %copy-start = (bf16[1,128,2048]{2,1,0:T(8,128)(2,1)S(1)}, bf16[1,128,2048]{2,1,0:T(8,128)(2,1)}, u32[]{:S(2)}) copy-start(bf16[1,128,2048]{2,1,0:T(8,128)(2,1)} %param.8) | copy-start | bytes 1572868
  6.5 123.9 %all-gather.13.cloned.1.call-start = ((), (), s32[]{:S(2)}) async-start(), calls=%async_computation.3 | async-start | bytes 2129920 | tf_op jit(solution)/shard_map/all_gather | solution.py:29
  8.0 219.5 %all-gather.11.cloned.1.call-start = ((), (), s32[]{:S(2)}) async-start(), calls=%async_computation.2 | async-start | bytes 1064960 | tf_op jit(solution)/shard_map/all_gather | solution.py:90
  8.7 347.6 %all-gather.15.cloned.1.call-start = ((), (), s32[]{:S(2)}) async-start(), calls=%async_computation.4 | async-start | bytes 2129920 | tf_op jit(solution)/shard_map/all_gather | solution.py:105
  9.5 473.2 %all-gather.17.cloned.1.call-start = ((), (), s32[]{:S(2)}) async-start(), calls=%async_computation.5 | async-start | bytes 4259840 | tf_op jit(solution)/shard_map/all_gather | solution.py:102
  10.0 599.6 %all-gather.19.cloned.1.call-start = ((), (), s32[]{:S(2)}) async-start(), calls=%async_computation.6 | async-start | bytes 4259840 | tf_op jit(solution)/shard_map/all_gather | solution.py:121
  14.1 219.3 %all-to-all-start = ((s32[64,1,4]{2,1,0:T(1,128)}), s32[64,1,4]{2,1,0:T(1,128)S(1)}, u32[]{:S(2)}, u32[]{:S(2)}) async-start(s32[64,1,4]{2,1,0:T(1,128)} %bitcast.4), calls=%async_computation | async-start | bytes 65536 | tf_op jit(solution)/shard_map/all_to_all | solution.py:95
  232.2 6.3 copy-start.1
  233.4 40.2 %all-to-all-start.1 = ((bf16[64,4,2048]{2,1,0:T(4,128)(2,1)}), bf16[64,4,2048]{2,1,0:T(4,128)(2,1)S(1)}, u32[]{:S(2)}, u32[]{:S(2)}) async-start(bf16[64,4,2048]{2,1,0:T(4,128)(2,1)} %reshape.254), calls=%async_computation.1 | async-start | bytes 2097152 | tf_op jit(solution)/shard_map/all_to_all | solution.py:94
  238.5 4.2 collective-permute-start.1
  358.4 3.9 collective-permute-start
  612.5 21.8 %collective-permute-start.2 = (bf16[128,2048]{1,0:T(8,128)(2,1)S(1)}, bf16[128,2048]{1,0:T(8,128)(2,1)S(1)}, u32[]{:S(2)}, u32[]{:S(2)}) collective-permute-start(bf16[128,2048]{1,0:T(8,128)(2,1)S(1)} %fusion.8), channel_id=1, source_target_pairs={{0,64},{64,128},{128,192},{192,256},{256,320},{320,384},{384,448},... | collective-permute-start | bytes 1572872 | tf_op jit(solution)/shard_map/ppermute | solution.py:21
Sparse Core Ops, SparseCore 0:
  11.8 118.6 all-gather.12
  135.0 92.4 all-gather.10
  231.9 124.3 all-gather.14
  360.7 121.9 all-gather.16
  487.1 122.4 all-gather.18
where the time goes:
time: 642 us
  waiting for transfers between devices  567 us (88%)
  starting transfers between devices  34.9 us (5%)
  between operations  13.4 us (2%)
  matrix products  12.8 us (2%)
  local copies, waits for them, and re-layouts  10.3 us (2%)
    all_gather x1, waiting for transfers between devices, on_device(): lax.all_gather(w_attn_out[0], 'dp', axis=0, tiled=True)  122 us
    all_gather x1, waiting for transfers between devices, on_device(): lax.all_gather(w_query[0], 'dp', axis=0, tiled=True)  120 us
    all_gather x1, waiting for transfers between devices, on_device(): lax.all_gather(w_patch_in[0], 'dp', axis=0, tiled=True)  97 us
    all_gather x1, waiting for transfers between devices, embed_rows(): lax.all_gather(w_out, 'dp', axis=0, tiled=True)  94.1 us
    all_gather x1, waiting for transfers between devices, on_device(): lax.all_gather(w_keyval[0], 'dp', axis=0, tiled=True)  80 us
    all_to_all x1, waiting for transfers between devices, on_device(): lax.all_to_all(outgoing, 'dp', split_axis=0, concat_axis=0, tiled=True)  29.6 us
    all_to_all x1, starting transfers between devices, on_device(): lax.all_to_all(places, 'dp', split_axis=0, concat_axis=0, tiled=True)  22.2 us
    ppermute x1, waiting for transfers between devices, from_behind(): lax.ppermute(x, axis, [(i, (i + by) % devices) for i in range(devices)])  19.8 us
  transfers between devices with their start and end apart: 10, of which 9 were waited for; matrix products, arithmetic and copies ran while one was open for 3% of the time, Pallas kernels for 0%

commit v1 on v0

v1 whole, which is shorter than its diff:
```python
import math

import jax
import jax.numpy as jnp
from jax import lax
from jax.experimental import pallas as pl
from jax.experimental.pallas import tpu as pltpu
from jax.sharding import PartitionSpec as P

HEADS = 16
KV_HEADS = 4
HEAD_WIDTH = 64
ROWS = 128
TAIL = 32
SLOTS = 4
PEERS = 64
MESH = pl.DeviceIdType.MESH
F32 = jnp.float32
BF16 = jnp.bfloat16
ALL = slice(None)


def iota(shape, dim):
    return lax.broadcasted_iota(jnp.int32, shape, dim)


def dot(a, b):
    return jnp.dot(a, b, preferred_element_type=F32)


def dot_nt(a, b):
    return lax.dot_general(a, b, (((1,), (1,)), ((), ())), preferred_element_type=F32)


def kernel(
    patches,
    dest,
    seg,
    w_in,
    w_out,
    w_query,
    w_keyval,
    w_proj,
    out,
    rows_v,
    g_in,
    g_out,
    g_qkv,
    g_proj,
    out_piece,
    sent,
    got,
    sent_at,
    got_at,
    segs,
    packed,
    tail,
    emb,
    normed,
    qkv,
    ctx,
    ss,
    rs,
    a2a_ss,
    a2a_rs,
    local,
):
    s = lax.axis_index("section")
    d = lax.axis_index("dp")
    h, x, y, c = d // 32, (d // 8) % 4, (d // 2) % 4, d % 2
    s_next, s_prev = (s + 1) % 8, (s + 7) % 8
    d_next, d_prev = (d + 1) % PEERS, (d + PEERS - 1) % PEERS
    x_by = {1: (x + 1) % 4, -1: (x + 3) % 4, 2: (x + 2) % 4}
    y_by = {1: (y + 1) % 4, -1: (y + 3) % 4, 2: (y + 2) % 4}
    z = h * 8 + s
    z_next, z_prev = (z + 1) % 16, (z + 15) % 16
    near, far = z_prev // 8, 1 - z_prev // 8

    def at(hh, xx, yy, cc):
        return hh * 32 + xx * 8 + yy * 2 + cc

    def x_peer(by):
        return (s, at(h, x_by[by], y, c))

    def y_peer(by):
        return (s, at(h, x, y_by[by], c))

    ahead = (s_next, at(z_next // 8, x, y, c))
    partner = (s, at(1 - h, x, y, c))
    sibling = (s, at(h, x, y, 1 - c))

    load_rows = pltpu.make_async_copy(patches, rows_v, local.at[0])
    load_rows.start()
    load_in = pltpu.make_async_copy(w_in, g_in.at[h, x, y, c], local.at[1])
    load_in.start()

    barrier = pltpu.get_barrier_semaphore()

    def greet(k, carry):
        pl.semaphore_signal(barrier, inc=1, device_id=(s_prev, k), device_id_type=MESH)
        return carry

    lax.fori_loop(0, PEERS, greet, 0)
    for peer in (
        partner,
        sibling,
        x_peer(1),
        x_peer(-1),
        y_peer(1),
        y_peer(-1),
        (s, d_prev),
    ):
        pl.semaphore_signal(barrier, inc=1, device_id=peer, device_id_type=MESH)

    wide = w_out[...].astype(F32)
    out_piece[...] = jnp.concatenate(
        [wide[:, 512 * j : 512 * (j + 1)] for j in range(4)], axis=0
    ).astype(BF16)

    to = dest[...]
    to_dev, to_slot = to // ROWS, to % ROWS
    match = (iota((PEERS, ROWS), 0) == to_dev).astype(F32)
    before = (iota((ROWS, ROWS), 0) < iota((ROWS, ROWS), 1)).astype(F32)
    earlier = dot(match.astype(BF16), before.astype(BF16))
    rank = jnp.sum(earlier * match, axis=0, keepdims=True).astype(jnp.int32)
    places = dot_nt(
        (match * (to_slot + 1).astype(F32)).astype(BF16),
        (iota((ROWS, ROWS), 0) % SLOTS == rank).astype(BF16),
    )
    sent_at[...] = (places.astype(jnp.int32) - 1).reshape(PEERS, 1, ROWS)
    line = iota((8 * PEERS, ROWS), 0)
    chosen = (line // 8 == to_dev) & (line % SLOTS == rank)
    pick_low = (chosen & (line % 8 < SLOTS)).astype(F32).astype(BF16)
    pick_high = (chosen & (line % 8 >= SLOTS)).astype(F32).astype(BF16)

    load_in.wait()
    pl.semaphore_wait(barrier, PEERS + 7)

    copies = []

    def send(src, dst, peer):
        i = len(copies)
        copy = pltpu.make_async_remote_copy(
            src_ref=src,
            dst_ref=dst,
            send_sem=ss.at[i],
            recv_sem=rs.at[i],
            device_id=peer,
            device_id_type=MESH,
        )
        copy.start()
        copies.append(copy)
        return copy

    def spread(ref, peer):
        return send(ref, ref, peer)

    in_far = spread(g_in.at[h, x, y, c], partner)
    out_near = send(out_piece, g_out.at[h, x, y, c], ahead)
    q_near = send(w_query, g_qkv.at[h, x, y, c, :, pl.ds(0, 1024)], ahead)
    kv_near = send(w_keyval, g_qkv.at[h, x, y, c, :, pl.ds(1024, 512)], ahead)
    o_near = send(w_proj, g_proj.at[h, x, y, c], ahead)
    seg_own = send(seg, segs.at[0], (s_next, d))
    seg_tail = send(seg, segs.at[1], (s_next, d_next))

    class Unit:
        def __init__(self, ref, hh):
            self.ref, self.hh = ref, hh
            self.width = ref.shape[-1]
            self.split = self.width >= 512
            self.core = []

        def block(self, lane, first, second, part=None):
            half = self.width // 2
            low, count = lane * half, half
            if part is not None and self.split:
                low, count = low + part * (half // 2), half // 2
            xx, yy = (first, second) if lane == 0 else (second, first)
            return self.ref.at[self.hh, xx, yy, c, :, pl.ds(low, count)]

        def one(self):
            self.c1 = {}
            for lane in (0, 1):
                a, b = (x, y) if lane == 0 else (y, x)
                peer = x_peer if lane == 0 else y_peer
                for way in (1, -1):
                    self.c1[lane, way] = spread(self.block(lane, a, b), peer(way))

        def forward(self, lane, way):
            return self.split or (way == 1) == (lane == 0)

        def two(self):
            self.c2 = {}
            for way in (1, -1):
                for lane in (0, 1):
                    by, b = (x_by, y) if lane == 0 else (y_by, x)
                    peer = x_peer if lane == 0 else y_peer
                    self.c1[lane, way].wait_recv()
                    if self.forward(lane, way):
                        self.c2[lane, way] = spread(
                            self.block(lane, by[-way], b, (1 - way) // 2), peer(way)
                        )

        def three(self):
            self.c3 = {}
            for lane in (0, 1):
                b = y if lane == 0 else x
                peer = y_peer if lane == 0 else x_peer
                for way in (1, -1):
                    if (lane, way) in self.c2:
                        self.c2[lane, way].wait_recv()
                whole = self.block(lane, ALL, b)
                for way in (1, -1):
                    self.c3[lane, way] = spread(whole, peer(way))
                self.core.append(spread(whole, sibling))

        def four(self):
            self.c4 = {}
            for way in (1, -1):
                for lane in (0, 1):
                    by = y_by if lane == 0 else x_by
                    peer = y_peer if lane == 0 else x_peer
                    self.c3[lane, way].wait_recv()
                    if self.forward(lane, way):
                        self.c4[lane, way] = spread(
                            self.block(lane, ALL, by[-way], (1 - way) // 2), peer(way)
                        )
                    self.core.append(spread(self.block(lane, ALL, by[-way]), sibling))

        def five(self):
            for lane in (0, 1):
                by = y_by if lane == 0 else x_by
                for way in (1, -1):
                    if (lane, way) in self.c4:
                        self.c4[lane, way].wait_recv()
                self.core.append(spread(self.block(lane, ALL, by[2]), sibling))

        def six(self):
            for copy in self.core:
                copy.wait_recv()

    u_in, u_out = Unit(g_in, ALL), Unit(g_out, ALL)
    u_qkv_n, u_qkv_f = Unit(g_qkv, near), Unit(g_qkv, far)
    u_o_n, u_o_f = Unit(g_proj, near), Unit(g_proj, far)

    def relay(ref, *arrived):
        for copy in arrived:
            copy.wait_recv()
        return spread(ref.at[near, x, y, c], partner)

    out_far = relay(g_out, out_near)
    qkv_far = relay(g_qkv, q_near, kv_near)
    in_far.wait_recv()
    u_in.one()
    u_qkv_n.one()
    o_far = relay(g_proj, o_near)

    u_in.two()
    u_qkv_n.two()
    u_in.three()
    u_qkv_n.three()
    u_in.four()
    out_far.wait_recv()
    u_out.one()
    u_o_n.one()
    u_in.five()
    u_qkv_n.four()
    u_out.two()
    u_o_n.two()

    load_rows.wait()
    u_in.six()
    first = jax.nn.gelu(dot(rows_v[...], g_in[...].reshape(2048, 256))).astype(BF16)
    picked = dot(pick_low, first[:, :128]) + dot(pick_high, first[:, 128:])
    sent[...] = picked.reshape(PEERS, 8, 128).astype(BF16)

    def exchange(k, carry):
        e = (d + k) % PEERS
        for src, dst, i in ((sent, got, 0), (sent_at, got_at, 1)):
            pltpu.make_async_remote_copy(
                src_ref=src.at[e],
                dst_ref=dst.at[d],
                send_sem=a2a_ss.at[i],
                recv_sem=a2a_rs.at[i],
                device_id=(s_next, e),
                device_id_type=MESH,
            ).start()
        return carry

    lax.fori_loop(0, PEERS, exchange, 0)

    u_out.three()
    u_o_n.three()
    qkv_far.wait_recv()
    u_qkv_f.one()
    u_qkv_n.five()
    u_out.four()
    u_o_n.four()
    u_qkv_f.two()
    o_far.wait_recv()
    u_o_f.one()
    u_out.five()
    u_o_n.five()
    u_qkv_f.three()
    u_o_f.two()

    pltpu.make_async_copy(got, got, a2a_rs.at[0]).wait()
    pltpu.make_async_copy(got_at, got_at, a2a_rs.at[1]).wait()
    place = got_at[...]
    source = iota((PEERS, 1, ROWS), 0)
    lane = iota((PEERS, 1, ROWS), 2)
    valued = [
        jnp.sum(jnp.where(source == (lane + ROWS * q) // 8, place, 0), axis=0)
        for q in range(4)
    ]
    valued = jnp.concatenate(valued, axis=1)
    column = iota((ROWS, 8 * PEERS), 1)
    put = iota((ROWS, 8 * PEERS), 0) == valued
    arrived = got[...].astype(F32).reshape(8 * PEERS, 128).astype(BF16)
    put_low = (put & (column % 8 < SLOTS)).astype(F32).astype(BF16)
    put_high = (put & (column % 8 >= SLOTS)).astype(F32).astype(BF16)
    packed[:, :128] = dot(put_low, arrived).astype(BF16)
    packed[:, 128:] = dot(put_high, arrived).astype(BF16)
    tail_copy = send(packed.at[pl.ds(ROWS - TAIL, TAIL)], tail, (s, d_next))

    u_qkv_f.four()
    u_o_f.three()

    tail_copy.wait_recv()
    u_out.six()
    both = jnp.concatenate([packed[...], tail[...]], axis=0)
    spreader = (
        iota((256, 1024), 0) == 4 * (iota((256, 1024), 1) // 16) + iota((256, 1024), 1) % 4
    )
    wide = dot(both, spreader.astype(F32).astype(BF16))
    group = (iota((ROWS + TAIL, 1024), 1) % 16) // 4
    for j in range(4):
        lhs = jnp.where(group == j, wide, 0.0).astype(BF16)
        emb[:, pl.ds(512 * j, 512)] = dot(lhs, g_out[...].reshape(1024, 512)).astype(BF16)
    residual = emb[...].astype(F32)
    scale = lax.rsqrt(jnp.mean(residual * residual, axis=-1, keepdims=True) + 1e-05)
    normed[...] = (residual * scale).astype(BF16)

    u_qkv_f.five()
    u_o_f.four()
    u_qkv_n.six()
    u_qkv_f.six()

    def project(j, carry):
        cols = pl.ds(pl.multiple_of(j * 256, 256), 256)
        weights = g_qkv[:, :, :, :, :, cols].reshape(2048, 256)
        qkv[:, cols] = dot(normed[...], weights).astype(BF16)
        return carry

    lax.fori_loop(0, 6, project, 0)

    seg_own.wait_recv()
    seg_tail.wait_recv()
    own = segs[0]
    square = iota((ROWS, ROWS), 0) == iota((ROWS, ROWS), 1)
    row_seg = jnp.sum(jnp.where(square, own, 0), axis=1, keepdims=True)
    key_seg = jnp.concatenate([own, pltpu.roll(segs[1], TAIL, 1)], axis=1)[:, : ROWS + TAIL]
    key = iota((ROWS, ROWS + TAIL), 1)
    row = iota((ROWS, ROWS + TAIL), 0)
    allowed = (key_seg == row_seg) & ((key <= row) | ((key >= ROWS) & (d > 0)))
    low = iota((ROWS + TAIL, 128), 1) < HEAD_WIDTH
    zero = jnp.zeros((ROWS + TAIL, 128), F32)

    def sides(tile, group):
        tile = tile.astype(F32)
        turned = pltpu.roll(tile, HEAD_WIDTH, 1)
        here, there = (tile, turned) if group == 0 else (turned, tile)
        return (
            jnp.where(low, here, zero).astype(BF16),
            jnp.where(low, zero, there).astype(BF16),
        )

    for pair in range(2):
        keys_tile = qkv[:, pl.ds(1024 + 128 * pair, 128)]
        values_tile = qkv[:, pl.ds(1280 + 128 * pair, 128)]
        for group in range(2):
            keys = sides(keys_tile, group)
            values = sides(values_tile, group)
            for tile in range(2):
                cols = 256 * (2 * pair + group) + 128 * tile
                queries = qkv[:ROWS, pl.ds(cols, 128)]
                total = None
                for side in range(2):
                    scores = dot_nt(queries, keys[side]) * (1.0 / math.sqrt(HEAD_WIDTH))
                    scores = jnp.where(allowed, scores, -jnp.inf)
                    expon = jnp.exp(scores - jnp.max(scores, axis=-1, keepdims=True))
                    probs = (expon / jnp.sum(expon, axis=-1, keepdims=True)).astype(BF16)
                    part = dot(probs, values[side])
                    total = part if total is None else total + part
                ctx[:, pl.ds(cols, 128)] = total.astype(BF16)

    u_o_f.five()
    u_o_n.six()
    u_o_f.six()

    def finish(j, carry):
        cols = pl.ds(pl.multiple_of(j * 256, 256), 256)
        weights = g_proj[:, :, :, :, :, cols].reshape(1024, 256)
        added = dot(ctx[...], weights) + emb[pl.ds(0, ROWS), cols].astype(F32)
        out[:, cols] = added.astype(BF16)
        return carry

    lax.fori_loop(0, 8, finish, 0)

    for copy in copies:
        copy.wait_send()
    pltpu.make_async_copy(sent, sent, a2a_ss.at[0]).wait()
    pltpu.make_async_copy(sent_at, sent_at, a2a_ss.at[1]).wait()


def on_device(patches, pack_dest, seg_ids, w_patch_in, w_patch_out, w_query, w_keyval, w_attn_out):
    vmem = pl.BlockSpec(memory_space=pltpu.VMEM)
    hbm = pl.BlockSpec(memory_space=pl.ANY)
    grid = (2, 4, 4, 2)
    out = pl.pallas_call(
        kernel,
        out_shape=jax.ShapeDtypeStruct((ROWS, 2048), BF16),
        in_specs=[hbm, vmem, vmem, hbm, vmem, hbm, hbm, hbm],
        out_specs=vmem,
        scratch_shapes=[
            pltpu.VMEM((ROWS, 2048), BF16),
            pltpu.VMEM(grid + (32, 256), BF16),
            pltpu.VMEM(grid + (16, 512), BF16),
            pltpu.VMEM(grid + (32, 1536), BF16),
            pltpu.VMEM(grid + (16, 2048), BF16),
            pltpu.VMEM((16, 512), BF16),
            pltpu.VMEM((PEERS, 8, 128), BF16),
            pltpu.VMEM((PEERS, 8, 128), BF16),
            pltpu.VMEM((PEERS, 1, ROWS), jnp.int32),
            pltpu.VMEM((PEERS, 1, ROWS), jnp.int32),
            pltpu.VMEM((2, 1, ROWS), jnp.int32),
            pltpu.VMEM((ROWS, 256), BF16),
            pltpu.VMEM((TAIL, 256), BF16),
            pltpu.VMEM((ROWS + TAIL, 2048), BF16),
            pltpu.VMEM((ROWS + TAIL, 2048), BF16),
            pltpu.VMEM((ROWS + TAIL, 1536), BF16),
            pltpu.VMEM((ROWS, 1024), BF16),
            pltpu.SemaphoreType.DMA((180,)),
            pltpu.SemaphoreType.DMA((180,)),
            pltpu.SemaphoreType.DMA((2,)),
            pltpu.SemaphoreType.DMA((2,)),
            pltpu.SemaphoreType.DMA((2,)),
        ],
        compiler_params=pltpu.CompilerParams(
            collective_id=0, has_side_effects=True, vmem_limit_bytes=48 << 20
        ),
        name="layer",
    )(
        patches[0],
        pack_dest,
        seg_ids,
        w_patch_in[0],
        w_patch_out[0],
        w_query[0],
        w_keyval[0],
        w_attn_out[0],
    )
    return out[None]


def solution(mesh):
    in_specs = (
        P("section", "dp", None),
        P("section", "dp"),
        P("section", "dp"),
        P("section", "dp", None),
        P("section", "dp", None),
        P("section", "dp", None),
        P("section", "dp", None),
        P("section", "dp", None),
    )
    out_specs = P("section", "dp", None)
    return jax.shard_map(
        on_device, mesh=mesh, in_specs=in_specs, out_specs=out_specs, check_vma=False
    )
```

time: 642 us -> 102 us (0.16)
  waiting for transfers between devices: 567 us -> 0 us
  Pallas kernels: 0 us -> 95.4 us
  starting transfers between devices: 34.9 us -> 0 us
  between operations: 13.4 us -> 0.02 us
  matrix products: 12.8 us -> 0 us
    all_gather x5 -> x0, waiting for transfers between devices: 513 us -> none  [the longest x1 122 us: on_device(): lax.all_gather(w_attn_out[0], 'dp', axis=0, tiled=True)]
    pallas_call x0 -> x1, Pallas kernels: none -> 95.4 us  [on_device(): pl.pallas_call(kernel, out_shape=jax.ShapeDtypeStruct((ROWS, 2048), BF16)...]
    all_to_all x2 -> x0, waiting for transfers between devices: 29.6 us -> none  [the longest x1 29.6 us: on_device(): lax.all_to_all(outgoing, 'dp', split_axis=0, concat_axis=0, tiled=True)]
    all_to_all x2 -> x0, starting transfers between devices: 27.3 us -> none  [the longest x1 22.2 us: on_device(): lax.all_to_all(places, 'dp', split_axis=0, concat_axis=0, tiled=True)]
    ppermute x3 -> x0, waiting for transfers between devices: 22.2 us -> none  [the longest x1 19.8 us: from_behind(): lax.ppermute(x, axis, [(i, (i + by) % devices) for i in range(devices)])]
    dot_general x5 -> x0, matrix products: 12 us -> none  [the longest x4 10.9 us: fold_columns(): return jnp.dot(left, shard_piece, preferred_element_type=jnp.float32)]
    ppermute x3 -> x0, starting transfers between devices: 7.46 us -> none  [the longest x2 5.54 us: shifted(): return lax.ppermute(block, axis, route)]
  transfers between devices with their start and end apart: 10 -> 0, of which waited for: 9 -> 0; matrix products, arithmetic and copies ran while one was open for 3% -> 0% of each run, Pallas kernels for 0% -> 0%
where the time goes in v1:
time: 102 us
  Pallas kernels  95.4 us (94%)
  local copies, waits for them, and re-layouts  6.38 us (6%)
    pallas_call x1, Pallas kernels, on_device(): pl.pallas_call(kernel, out_shape=jax.ShapeDtypeStruct((ROWS, 2048), BF16)...  95.4 us
    unnamed x17, local copies, waits for them, and re-layouts  6.38 us

profile of v1, /device:TPU:1, one launch (start us, length us, event | category | flops | bytes accessed | tf_op | source)
XLA Modules:
  0.0 101.8 jit_solution(4017786130261914248)
XLA Ops:
  0.0 0.0 copy-start.6
  0.0 0.0 copy-start.7
  0.0 0.7 copy-done.6
  0.7 0.0 copy-done.7
  0.7 0.0 copy-start
  0.7 1.0 %copy-done = bf16[1,128,2048]{2,1,0:T(8,128)(2,1)S(1)} copy-done((bf16[1,128,2048]{2,1,0:T(8,128)(2,1)S(1)}, bf16[1,128,2048]{2,1,0:T(8,128)(2,1)}, u32[]{:S(2)}) %copy-start) | copy-done | bytes 524312
  1.7 0.0 copy-start.1
  1.7 0.8 copy-done.1
  2.6 0.0 copy-start.2
  2.6 0.8 copy-done.2
  3.4 0.0 copy-start.3
  3.4 0.8 copy-done.3
  4.2 0.0 copy-start.4
  4.2 0.7 copy-done.4
  4.9 0.0 copy-start.5
  4.9 0.7 copy-done.5
  5.6 95.4 %layer.1 = bf16[128,2048]{1,0:T(8,128)(2,1)S(1)} custom-call(bf16[128,2048]{1,0:T(8,128)(2,1)S(1)} %bitcast.8, s32[1,128]{1,0:T(1,128)S(1)} %copy-done.6, s32[1,128]{1,0:T(1,128)S(1)} %copy-done.7, bf16[32,256]{1,0:T(8,128)(2,1)S(1)} %bitcast.12, bf16[4,2048]{1,0:T(4,128)(2,1)S(1)} %bitcast.13, bf16[32,1024]{1,0:T(8,128)(2,1)S(1)} %bitcast.9, ...), custom_call_target="tpu_custom_call" | custom-call | tf_op jit(solution)/shard_map/layer/pallas_call | solution.py:420
  101.0 0.8 copy.10
Async XLA Ops:
  0.0 0.7 copy-start.6
  0.0 0.7 copy-start.7
  0.7 1.0 %copy-start = (bf16[1,128,2048]{2,1,0:T(8,128)(2,1)S(1)}, bf16[1,128,2048]{2,1,0:T(8,128)(2,1)}, u32[]{:S(2)}) copy-start(bf16[1,128,2048]{2,1,0:T(8,128)(2,1)} %param.8) | copy-start | bytes 1572868
  1.7 0.8 copy-start.1
  2.6 0.8 copy-start.2
  3.4 0.8 copy-start.3
  4.2 0.7 copy-start.4
  4.9 0.7 copy-start.5

commit v2 on v1

v2 whole, which is shorter than its diff:
```python
import math

import jax
import jax.numpy as jnp
from jax import lax
from jax.experimental import pallas as pl
from jax.experimental.pallas import tpu as pltpu
from jax.sharding import PartitionSpec as P

HEADS = 16
KV_HEADS = 4
HEAD_WIDTH = 64
ROWS = 128
TAIL = 32
SLOTS = 4
PEERS = 64
MESH = pl.DeviceIdType.MESH
F32 = jnp.float32
BF16 = jnp.bfloat16
ALL = slice(None)


def iota(shape, dim):
    return lax.broadcasted_iota(jnp.int32, shape, dim)


def dot(a, b):
    return jnp.dot(a, b, preferred_element_type=F32)


def dot_nt(a, b):
    return lax.dot_general(a, b, (((1,), (1,)), ((), ())), preferred_element_type=F32)


def kernel(
    patches,
    dest_hbm,
    seg_hbm,
    w_in,
    w_out_hbm,
    w_query,
    w_keyval,
    w_proj,
    out,
    dest,
    seg,
    w_out,
    rows_v,
    g_in,
    g_out,
    g_qkv,
    g_proj,
    out_piece,
    held_qkv,
    held_o,
    sent,
    got,
    packed,
    tail,
    emb,
    normed,
    qkv,
    ctx,
    ss,
    rs,
    a2a_ss,
    a2a_rs,
    local,
    ready,
):
    s = lax.axis_index("section")
    d = lax.axis_index("dp")
    h, x, y, c = d // 32, (d // 8) % 4, (d // 2) % 4, d % 2
    s_next, s_prev = (s + 1) % 8, (s + 7) % 8
    d_next = (d + 1) % PEERS
    x_by = {1: (x + 1) % 4, -1: (x + 3) % 4, 2: (x + 2) % 4}
    y_by = {1: (y + 1) % 4, -1: (y + 3) % 4, 2: (y + 2) % 4}
    z = h * 8 + s
    z_next, z_prev = (z + 1) % 16, (z + 15) % 16
    near, far = z_prev // 8, 1 - z_prev // 8

    def at(hh, xx, yy, cc):
        return hh * 32 + xx * 8 + yy * 2 + cc

    def x_peer(by):
        return (s, at(h, x_by[by], y, c))

    def y_peer(by):
        return (s, at(h, x, y_by[by], c))

    ahead = (s_next, at(z_next // 8, x, y, c))
    across = (s_next, at(1 - z_next // 8, x, y, c))
    behind = (s_prev, at(near, x, y, c))
    behind_across = (s_prev, at(far, x, y, c))
    four_up = ((s + 4) % 8, at((z + 4) % 16 // 8, x, y, c))
    four_down = ((s + 4) % 8, at((z + 12) % 16 // 8, x, y, c))
    relayed = (z + 11) % 16 // 8
    partner = (s, at(1 - h, x, y, c))
    sibling = (s, at(h, x, y, 1 - c))

    loads = [
        pltpu.make_async_copy(src, dst, local.at[i])
        for i, (src, dst) in enumerate(
            (
                (w_in, g_in.at[h, x, y, c]),
                (w_out_hbm, w_out),
                (dest_hbm, dest),
                (seg_hbm, seg),
                (patches, rows_v),
            )
        )
    ]
    for load in loads:
        load.start()

    barrier = pltpu.get_barrier_semaphore()

    near_by = (behind, behind_across, four_down, partner, sibling)
    near_by += tuple(map(x_peer, (1, -1, 2))) + tuple(map(y_peer, (1, -1, 2)))
    for peer in near_by:
        pl.semaphore_signal(barrier, inc=1, device_id=peer, device_id_type=MESH)

    for load in loads[:4]:
        load.wait()
    wide = w_out[...].astype(F32)
    out_piece[:, :512] = jnp.concatenate(
        [wide[:, 512 * j : 512 * (j + 1)] for j in range(4)], axis=0
    ).astype(BF16)
    to = dest[...]
    to_dev, to_slot = to // ROWS, to % ROWS
    note = iota((16, ROWS), 0)
    out_piece[:, 512:] = jnp.where(
        note == 0, to_dev, jnp.where(note == 1, to_slot, jnp.where(note == 2, seg[...], 0))
    ).astype(F32).astype(BF16)

    match = (iota((PEERS, ROWS), 0) == to_dev).astype(F32)
    before = (iota((ROWS, ROWS), 0) < iota((ROWS, ROWS), 1)).astype(F32).astype(BF16)
    earlier = dot(match.astype(BF16), before)
    rank = jnp.sum(earlier * match, axis=0, keepdims=True).astype(jnp.int32)
    line = iota((8 * PEERS, ROWS), 0)
    chosen = (line // 8 == to_dev) & (line % SLOTS == rank)
    pick_low = (chosen & (line % 8 < SLOTS)).astype(F32).astype(BF16)
    pick_high = (chosen & (line % 8 >= SLOTS)).astype(F32).astype(BF16)

    pl.semaphore_wait(barrier, len(near_by))

    copies = []

    def send(src, dst, peer):
        i = len(copies)
        copy = pltpu.make_async_remote_copy(
            src_ref=src,
            dst_ref=dst,
            send_sem=ss.at[i],
            recv_sem=rs.at[i],
            device_id=peer,
            device_id_type=MESH,
        )
        copy.start()
        copies.append(copy)
        return copy

    def spread(ref, peer):
        return send(ref, ref, peer)

    in_far = spread(g_in.at[h, x, y, c], partner)
    mine = g_qkv.at[h, x, y, c]
    mine, mine_o = g_qkv.at[h, x, y, c], g_proj.at[h, x, y, c]
    low, high = pl.ds(0, 768), pl.ds(768, 768)
    left, right = pl.ds(0, 1024), pl.ds(1024, 1024)
    low_far = send(w_query.at[:, low], mine.at[:, low], across)
    high_near = send(w_query.at[:, pl.ds(768, 256)], mine.at[:, pl.ds(768, 256)], ahead)
    kv_near = send(w_keyval, mine.at[:, pl.ds(1024, 512)], ahead)
    out_far = send(out_piece, g_out.at[h, x, y, c], across)
    low_near = send(w_query.at[:, low], mine.at[:, low], ahead)
    left_far = send(w_proj.at[:, left], mine_o.at[:, left], across)
    o_near = send(w_proj, mine_o, ahead)
    out_near = send(out_piece, g_out.at[h, x, y, c], ahead)

    class Unit:
        def __init__(self, ref, hh):
            self.ref, self.hh = ref, hh
            self.width = ref.shape[-1]
            self.split = self.width > 640
            self.ways = (1, -1) if self.split else (1, -1, 2)
            self.core, self.c1 = [], {}

        def block(self, lane, first, second, part=None):
            low, count = (0, 256) if lane == 0 else (256, 384)
            if self.width != 640:
                half = self.width // 2
                low, count = lane * half, half
            if part is not None:
                low, count = low + part * (half // 2), half // 2
            xx, yy = (first, second) if lane == 0 else (second, first)
            return self.ref.at[self.hh, xx, yy, c, :, pl.ds(low, count)]

        def one(self, lanes=(0, 1)):
            for way in (1, -1, 2):
                for lane in lanes:
                    a, b = (x, y) if lane == 0 else (y, x)
                    peer = x_peer if lane == 0 else y_peer
                    self.c1[lane, way] = spread(self.block(lane, a, b), peer(way))

        def three(self):
            self.c3 = {}
            for lane in (0, 1):
                b = y if lane == 0 else x
                peer = y_peer if lane == 0 else x_peer
                for way in (1, -1, 2):
                    self.c1[lane, way].wait_recv()
                whole = self.block(lane, ALL, b)
                for way in self.ways:
                    self.c3[lane, way] = spread(whole, peer(way))
                if self.split:
                    self.core.append(spread(whole, sibling))

        def four(self):
            self.c4 = {}
            for way in (1, -1):
                for lane in (0, 1):
                    by = y_by if lane == 0 else x_by
                    peer = y_peer if lane == 0 else x_peer
                    self.c3[lane, way].wait_recv()
                    self.c4[lane, way] = spread(
                        self.block(lane, ALL, by[-way], (1 - way) // 2), peer(way)
                    )
                    self.core.append(spread(self.block(lane, ALL, by[-way]), sibling))

        def five(self):
            for copy in (self.c4 if self.split else self.c3).values():
                copy.wait_recv()
            if not self.split:
                self.core.append(spread(self.ref.at[self.hh, :, :, c], sibling))
                return
            for lane in (0, 1):
                by = y_by if lane == 0 else x_by
                self.core.append(spread(self.block(lane, ALL, by[2]), sibling))

        def six(self):
            for copy in self.core:
                copy.wait_recv()

    u_in, u_out = Unit(g_in, ALL), Unit(g_out, ALL)
    u_qkv_n, u_qkv_f = Unit(g_qkv, near), Unit(g_qkv, far)
    u_o_n, u_o_f = Unit(g_proj, near), Unit(g_proj, far)

    high_near.wait_recv()
    kv_near.wait_recv()
    high_up = send(g_qkv.at[near, x, y, c, :, high], held_qkv, four_up)
    low_near.wait_recv()
    u_qkv_n.one()
    in_far.wait_recv()
    u_in.one()
    o_near.wait_recv()
    right_up = send(g_proj.at[near, x, y, c, :, right], held_o, four_up)
    u_o_n.one()
    u_in.three()
    u_qkv_n.three()
    high_up.wait_recv()
    high_far = send(held_qkv, g_qkv.at[relayed, x, y, c, :, high], four_up)
    out_near.wait_recv()
    out_far.wait_recv()
    u_out.one()
    u_in.five()
    right_up.wait_recv()
    right_far = send(held_o, g_proj.at[relayed, x, y, c, :, right], four_up)
    u_o_n.three()
    u_out.three()

    loads[4].wait()
    u_in.six()
    pl.semaphore_signal(ready, inc=1, device_id=behind, device_id_type=MESH)
    first = jax.nn.gelu(dot(rows_v[...], g_in[...].reshape(2048, 256))).astype(BF16)
    picked = dot(pick_low, first[:, :128]) + dot(pick_high, first[:, 128:])
    sent[...] = picked.reshape(PEERS, 8, 128).astype(BF16)

    def exchange(plane):
        def to_one(k, carry):
            e = plane * 32 + (d + k) % 32
            pltpu.make_async_remote_copy(
                src_ref=sent.at[e],
                dst_ref=got.at[d],
                send_sem=a2a_ss,
                recv_sem=a2a_rs,
                device_id=(s_next, e),
                device_id_type=MESH,
            ).start()
            return carry

        lax.fori_loop(0, 32, to_one, 0)

    pl.semaphore_wait(ready, 1)
    exchange(1 - z_next // 8)
    exchange(z_next // 8)

    low_far.wait_recv()
    u_qkv_f.one((0,))
    u_qkv_n.four()
    high_far.wait_recv()
    u_qkv_f.one((1,))
    u_o_n.four()
    left_far.wait_recv()
    u_o_f.one((0,))
    u_out.five()
    u_qkv_f.three()
    right_far.wait_recv()
    u_o_f.one((1,))
    u_qkv_n.five()
    u_o_n.five()
    u_o_f.three()

    u_out.six()
    wanted = iota((144, 1024), 0)
    line = iota((144, 1024), 1)
    owner = jnp.where(wanted < 128, wanted % PEERS, jnp.where(wanted == 128, d, (d + 63) % PEERS))
    kind = jnp.where(wanted < 64, 0, jnp.where(wanted < 128, 1, 2))
    notes = dot(
        (line == 16 * owner + kind).astype(F32).astype(BF16),
        g_out[:, :, :, :, :, pl.ds(512, 128)].reshape(1024, 128),
    )
    own, seg_before = notes[128:129], notes[129:130]
    here = (notes[:64] == d.astype(F32)).astype(F32)
    earlier = dot(here.astype(BF16), before)
    spot = here * (notes[64:128] + 1.0)
    line = iota((PEERS, 8 * PEERS), 1)
    valued = jnp.zeros((PEERS, 8 * PEERS), F32)
    for k in range(SLOTS):
        value = jnp.sum(jnp.where(earlier == float(k), spot, 0.0), axis=1, keepdims=True)
        valued = jnp.where(line % SLOTS == k, value, valued)
    valued = jnp.where(line // 8 == iota((PEERS, 8 * PEERS), 0), valued, 0.0)
    valued = jnp.sum(valued, axis=0, keepdims=True)
    put = iota((ROWS, 8 * PEERS), 0).astype(F32) + 1.0 == valued
    column = iota((ROWS, 8 * PEERS), 1)
    put_low = (put & (column % 8 < SLOTS)).astype(F32).astype(BF16)
    put_high = (put & (column % 8 >= SLOTS)).astype(F32).astype(BF16)

    u_qkv_f.four()
    pltpu.make_async_copy(got, got, a2a_rs).wait()
    arrived = got[...].astype(F32).reshape(8 * PEERS, 128).astype(BF16)
    packed[:, :128] = dot(put_low, arrived).astype(BF16)
    packed[:, 128:] = dot(put_high, arrived).astype(BF16)
    tail_copy = send(packed.at[pl.ds(ROWS - TAIL, TAIL)], tail, (s, d_next))
    u_o_f.four()

    spreader = (
        iota((256, 1024), 0) == 4 * (iota((256, 1024), 1) // 16) + iota((256, 1024), 1) % 4
    )
    spreader = spreader.astype(F32).astype(BF16)

    def embed(rows, start, count):
        wide = dot(rows, spreader)
        group = (iota((count, 1024), 1) % 16) // 4
        for j in range(4):
            lhs = jnp.where(group == j, wide, 0.0).astype(BF16)
            weights = g_out[:, :, :, :, :, pl.ds(0, 512)].reshape(1024, 512)
            emb[pl.ds(start, count), pl.ds(512 * j, 512)] = dot(lhs, weights).astype(BF16)
        residual = emb[pl.ds(start, count)].astype(F32)
        scale = lax.rsqrt(jnp.mean(residual * residual, axis=-1, keepdims=True) + 1e-05)
        normed[pl.ds(start, count)] = (residual * scale).astype(BF16)

    embed(packed[...], 0, ROWS)
    u_qkv_f.five()
    tail_copy.wait_recv()
    embed(tail[...], ROWS, TAIL)
    u_qkv_n.six()
    u_qkv_f.six()

    def project(j, carry):
        cols = pl.ds(pl.multiple_of(j * 256, 256), 256)
        weights = g_qkv[:, :, :, :, :, cols].reshape(2048, 256)
        qkv[:, cols] = dot(normed[...], weights).astype(BF16)
        return carry

    lax.fori_loop(0, 6, project, 0)
    u_o_f.five()

    square = iota((ROWS, ROWS), 0) == iota((ROWS, ROWS), 1)
    row_seg = jnp.sum(jnp.where(square, own, 0.0), axis=1, keepdims=True)
    key_seg = jnp.concatenate([own, pltpu.roll(seg_before, TAIL, 1)], axis=1)[:, : ROWS + TAIL]
    key = iota((ROWS, ROWS + TAIL), 1)
    row = iota((ROWS, ROWS + TAIL), 0)
    allowed = (key_seg == row_seg) & ((key <= row) | ((key >= ROWS) & (d > 0)))
    low = iota((ROWS + TAIL, 128), 1) < HEAD_WIDTH
    zero = jnp.zeros((ROWS + TAIL, 128), F32)

    def sides(tile, group):
        tile = tile.astype(F32)
        turned = pltpu.roll(tile, HEAD_WIDTH, 1)
        here, there = (tile, turned) if group == 0 else (turned, tile)
        return (
            jnp.where(low, here, zero).astype(BF16),
            jnp.where(low, zero, there).astype(BF16),
        )

    for pair in range(2):
        keys_tile = qkv[:, pl.ds(1024 + 128 * pair, 128)]
        values_tile = qkv[:, pl.ds(1280 + 128 * pair, 128)]
        for group in range(2):
            keys = sides(keys_tile, group)
            values = sides(values_tile, group)
            for tile in range(2):
                cols = 256 * (2 * pair + group) + 128 * tile
                queries = qkv[:ROWS, pl.ds(cols, 128)]
                total = None
                for side in range(2):
                    scores = dot_nt(queries, keys[side]) * (1.0 / math.sqrt(HEAD_WIDTH))
                    scores = jnp.where(allowed, scores, -jnp.inf)
                    expon = jnp.exp(scores - jnp.max(scores, axis=-1, keepdims=True))
                    probs = (expon / jnp.sum(expon, axis=-1, keepdims=True)).astype(BF16)
                    part = dot(probs, values[side])
                    total = part if total is None else total + part
                ctx[:, pl.ds(cols, 128)] = total.astype(BF16)

    u_o_n.six()
    u_o_f.six()

    def finish(j, carry):
        cols = pl.ds(pl.multiple_of(j * 256, 256), 256)
        weights = g_proj[:, :, :, :, :, cols].reshape(1024, 256)
        added = dot(ctx[...], weights) + emb[pl.ds(0, ROWS), cols].astype(F32)
        out[:, cols] = added.astype(BF16)
        return carry

    lax.fori_loop(0, 8, finish, 0)

    for copy in copies:
        copy.wait_send()
    pltpu.make_async_copy(sent, sent, a2a_ss).wait()


def on_device(patches, pack_dest, seg_ids, w_patch_in, w_patch_out, w_query, w_keyval, w_attn_out):
    vmem = pl.BlockSpec(memory_space=pltpu.VMEM)
    hbm = pl.BlockSpec(memory_space=pltpu.HBM)
    grid = (2, 4, 4, 2)
    out = pl.pallas_call(
        kernel,
        out_shape=jax.ShapeDtypeStruct((ROWS, 2048), BF16),
        in_specs=[hbm] * 8,
        out_specs=vmem,
        scratch_shapes=[
            pltpu.VMEM((1, ROWS), jnp.int32),
            pltpu.VMEM((1, ROWS), jnp.int32),
            pltpu.VMEM((4, 2048), BF16),
            pltpu.VMEM((ROWS, 2048), BF16),
            pltpu.VMEM(grid + (32, 256), BF16),
            pltpu.VMEM(grid + (16, 640), BF16),
            pltpu.VMEM(grid + (32, 1536), BF16),
            pltpu.VMEM(grid + (16, 2048), BF16),
            pltpu.VMEM((16, 640), BF16),
            pltpu.VMEM((32, 768), BF16),
            pltpu.VMEM((16, 1024), BF16),
            pltpu.VMEM((PEERS, 8, 128), BF16),
            pltpu.VMEM((PEERS, 8, 128), BF16),
            pltpu.VMEM((ROWS, 256), BF16),
            pltpu.VMEM((TAIL, 256), BF16),
            pltpu.VMEM((ROWS + TAIL, 2048), BF16),
            pltpu.VMEM((ROWS + TAIL, 2048), BF16),
            pltpu.VMEM((ROWS + TAIL, 1536), BF16),
            pltpu.VMEM((ROWS, 1024), BF16),
            pltpu.SemaphoreType.DMA((180,)),
            pltpu.SemaphoreType.DMA((180,)),
            pltpu.SemaphoreType.DMA,
            pltpu.SemaphoreType.DMA,
            pltpu.SemaphoreType.DMA((5,)),
            pltpu.SemaphoreType.REGULAR,
        ],
        compiler_params=pltpu.CompilerParams(
            collective_id=0, has_side_effects=True, vmem_limit_bytes=64 << 20
        ),
        name="layer",
    )(
        patches[0],
        pack_dest,
        seg_ids,
        w_patch_in[0],
        w_patch_out[0],
        w_query[0],
        w_keyval[0],
        w_attn_out[0],
    )
    return out[None]


def solution(mesh):
    in_specs = (
        P("section", "dp", None),
        P("section", "dp"),
        P("section", "dp"),
        P("section", "dp", None),
        P("section", "dp", None),
        P("section", "dp", None),
        P("section", "dp", None),
        P("section", "dp", None),
    )
    out_specs = P("section", "dp", None)
    return jax.shard_map(
        on_device, mesh=mesh, in_specs=in_specs, out_specs=out_specs, check_vma=False
    )
```

time: 102 us -> 80.3 us (0.79)
  Pallas kernels: 95.4 us -> 78.3 us
  local copies, waits for them, and re-layouts: 6.38 us -> 1.88 us
    pallas_call x1, Pallas kernels: 95.4 us -> 78.3 us  [on_device(): pl.pallas_call(kernel, out_shape=jax.ShapeDtypeStruct((ROWS, 2048), BF16)...]
    unnamed x17 -> x1, local copies, waits for them, and re-layouts: 6.38 us -> 1.88 us
where the time goes in v2:
time: 80.3 us; the launch traced here: 80.2 us
  Pallas kernels  78.3 us (98%)
  local copies, waits for them, and re-layouts  1.88 us (2%)
    pallas_call x1, Pallas kernels, on_device(): pl.pallas_call(kernel, out_shape=jax.ShapeDtypeStruct((ROWS, 2048), BF16)...  78.3 us
    unnamed x1, local copies, waits for them, and re-layouts  1.88 us

profile of v2, /device:TPU:1, one launch (start us, length us, event | category | flops | bytes accessed | tf_op | source)
XLA Modules:
  0.0 80.2 jit_solution(758019240468228181)
XLA Ops:
  0.0 78.3 %layer.1 = bf16[128,2048]{1,0:T(8,128)(2,1)} custom-call(bf16[128,2048]{1,0:T(8,128)(2,1)} %bitcast.8, s32[1,128]{1,0:T(1,128)} %dest_hbm.1, s32[1,128]{1,0:T(1,128)} %seg_hbm.1, bf16[32,256]{1,0:T(8,128)(2,1)} %bitcast.12, bf16[4,2048]{1,0:T(4,128)(2,1)} %bitcast.13, bf16[32,1024]{1,0:T(8,128)(2,1)} %bitcast.9, bf16[32,512]{1,0:T(8,128)(2,1)} %bitcast.11, ...), custom_call_target="tpu_custom_call" | custom-call | tf_op jit(solution)/shard_map/layer/pallas_call | solution.py:436
  78.3 1.9 %copy.10 = bf16[1,128,2048]{2,1,0:T(8,128)(2,1)} copy(bf16[1,128,2048]{2,1,0:T(8,128)(2,1)} %bitcast.7) | data formatting | bytes 1048576

commit v3 on v2

--- a/solution.py
+++ b/solution.py
@@ -61,6 +61,7 @@
     normed,
     qkv,
     ctx,
+    partial,
     ss,
     rs,
     a2a_ss,
@@ -182,7 +183,7 @@
             self.ref, self.hh = ref, hh
             self.width = ref.shape[-1]
             self.split = self.width > 640
-            self.ways = (1, -1) if self.split else (1, -1, 2)
+            self.ways = (1, -1) if self.split else (2, 1, -1)
             self.core, self.c1 = [], {}
 
         def block(self, lane, first, second, part=None):
@@ -196,7 +197,7 @@
             return self.ref.at[self.hh, xx, yy, c, :, pl.ds(low, count)]
 
         def one(self, lanes=(0, 1)):
-            for way in (1, -1, 2):
+            for way in (2, 1, -1):
                 for lane in lanes:
                     a, b = (x, y) if lane == 0 else (y, x)
                     peer = x_peer if lane == 0 else y_peer
@@ -412,17 +413,24 @@
                     total = part if total is None else total + part
                 ctx[:, pl.ds(cols, 128)] = total.astype(BF16)
 
+    def half(hh, cols):
+        context = ctx[:, pl.ds(pl.multiple_of(hh * 512, 512), 512)]
+        return dot(context, g_proj[hh, :, :, :, :, cols].reshape(512, 512))
+
+    def begin(j, carry):
+        cols = pl.ds(pl.multiple_of(j * 512, 512), 512)
+        partial[:, cols] = half(near, cols) + emb[pl.ds(0, ROWS), cols].astype(F32)
+        return carry
+
+    def finish(j, carry):
+        cols = pl.ds(pl.multiple_of(j * 512, 512), 512)
+        out[:, cols] = (partial[:, cols] + half(far, cols)).astype(BF16)
+        return carry
+
     u_o_n.six()
+    lax.fori_loop(0, 4, begin, 0)
     u_o_f.six()
-
-    def finish(j, carry):
-        cols = pl.ds(pl.multiple_of(j * 256, 256), 256)
-        weights = g_proj[:, :, :, :, :, cols].reshape(1024, 256)
-        added = dot(ctx[...], weights) + emb[pl.ds(0, ROWS), cols].astype(F32)
-        out[:, cols] = added.astype(BF16)
-        return carry
-
-    lax.fori_loop(0, 8, finish, 0)
+    lax.fori_loop(0, 4, finish, 0)
 
     for copy in copies:
         copy.wait_send()
@@ -458,6 +466,7 @@
             pltpu.VMEM((ROWS + TAIL, 2048), BF16),
             pltpu.VMEM((ROWS + TAIL, 1536), BF16),
             pltpu.VMEM((ROWS, 1024), BF16),
+            pltpu.VMEM((ROWS, 2048), F32),
             pltpu.SemaphoreType.DMA((180,)),
             pltpu.SemaphoreType.DMA((180,)),
             pltpu.SemaphoreType.DMA,

time: 80.3 us -> 79.4 us (0.989)
  Pallas kernels: 78.3 us -> 77.3 us
    pallas_call x1, Pallas kernels: 78.3 us -> 77.3 us  [on_device(): pl.pallas_call(kernel, out_shape=jax.ShapeDtypeStruct((ROWS, 2048), BF16)...]
where the time goes in v3:
time: 79.4 us; the launch traced here: 79.2 us
  Pallas kernels  77.3 us (97%)
  local copies, waits for them, and re-layouts  1.88 us (2%)
    pallas_call x1, Pallas kernels, on_device(): pl.pallas_call(kernel, out_shape=jax.ShapeDtypeStruct((ROWS, 2048), BF16)...  77.3 us
    unnamed x1, local copies, waits for them, and re-layouts  1.88 us

profile of v3, /device:TPU:1, one launch (start us, length us, event | category | flops | bytes accessed | tf_op | source)
XLA Modules:
  0.0 79.2 jit_solution(17548402311023244002)
XLA Ops:
  0.0 77.3 %layer.1 = bf16[128,2048]{1,0:T(8,128)(2,1)} custom-call(bf16[128,2048]{1,0:T(8,128)(2,1)} %bitcast.8, s32[1,128]{1,0:T(1,128)} %dest_hbm.1, s32[1,128]{1,0:T(1,128)} %seg_hbm.1, bf16[32,256]{1,0:T(8,128)(2,1)} %bitcast.12, bf16[4,2048]{1,0:T(4,128)(2,1)} %bitcast.13, bf16[32,1024]{1,0:T(8,128)(2,1)} %bitcast.9, bf16[32,512]{1,0:T(8,128)(2,1)} %bitcast.11, ...), custom_call_target="tpu_custom_call" | custom-call | tf_op jit(solution)/shard_map/layer/pallas_call | solution.py:444
  77.3 1.9 %copy.10 = bf16[1,128,2048]{2,1,0:T(8,128)(2,1)} copy(bf16[1,128,2048]{2,1,0:T(8,128)(2,1)} %bitcast.7) | data formatting | bytes 1048576
